TPU v7x, 32 devices: a whole 2x2x4 slice. The times are simulated.
32 devices in a mesh: groups: 2 (over y), seq: 4 (over z), fsdp: 2 (over x), head: 2 (over core).
Axes of the slice: x: 2, y: 2, z: 4, core: 2. Of those that a mesh axis runs over, the one named last changes fastest.
Arguments:
- frames: bfloat16 [6144, 3072], P(('groups', 'seq')), parts along dimension 0, may hold values from -330 to 330
- modulation: float32 [4, 3072], P('groups'), parts along dimension 0, may hold values from -2.5 to 2.5
- w_qkv: bfloat16 [3072, 3, 2048], P('seq', None, ('fsdp', 'head')), may hold values from -0.109375 to 0.109375
- b_qkv: float32 [3, 2048], P(None, ('fsdp', 'head')), may hold values from -2.5 to 2.5
- qk_gain: float32 [2, 128], replicated, may hold values from 0.7 to 2.4
- block_lists: int32 [16, 27], P(('groups', 'seq')), parts along dimension 0, may hold values from -1 to 7, as said below
Outputs:
- attention: bfloat16 [6144, 2048], P(('groups', 'seq'), ('fsdp', 'head')), parts along dimension 0
There are 2 independent parts, one for each index of `groups`. A program takes and returns all parts, laid end to end along the dimension named above; an argument that names none is the same for every part. Nothing has to cross between parts.
Inputs may be any that keep to these rules, and one draw needn't show every extreme that they name: `block_lists`: tile g lies at width g // 2, time (g % 2) // 1 and height g % 1 of a 2 x 1 x 4 grid of tiles. Entry (a + 1) * 9 + (b + 1) * 3 + (c + 1) of row g, for a, b, c in -1, 0, 1, is the tile at time + a, height + b and width + c of tile g, or -1 where that tile is outside the grid or left out of the list. Entry 13 is always g.
All inputs are finite; a program needn't handle non-finite values.
Results may differ from a plain program's by a relative error of at most 0.0058.
Values may be sent and summed in bfloat16 or wider, within the bound.
No kernel may reach another device: no remote copies, remote signals or barrier semaphores. Data moves between devices by JAX's collectives and lax.ppermute only.
A program may use at most 128 MiB of HBM per device.

v0:
```python
import math
import jax
import jax.numpy as jnp
from jax import lax
from jax.sharding import PartitionSpec as P


def with_halo(shard, sides, width):
    for axis, dim in sides:
        devices, length = (lax.axis_size(axis), shard.shape[dim])
        up = [(i, (i + 1) % devices) for i in range(devices - 1)]
        down = [(j, i) for i, j in up]
        last = lax.slice_in_dim(shard, length - width, length, axis=dim)
        first = lax.slice_in_dim(shard, 0, width, axis=dim)
        before = lax.ppermute(last, axis, up)
        after = lax.ppermute(first, axis, down)
        shard = jnp.concatenate([before, shard, after], axis=dim)
    return shard


def normed_heads(tensor, gain_row, head_dim):
    shaped = tensor.reshape(tensor.shape[0], tensor.shape[1] // head_dim, head_dim)
    scaled = (
        shaped * lax.rsqrt(jnp.mean(shaped * shaped, axis=-1, keepdims=True) + 1e-06) * gain_row
    )
    return scaled.astype(jnp.bfloat16)


def reach_sides(key_rows, values):
    stacked = jnp.stack([key_rows, values], axis=0)
    return with_halo(stacked, (("seq", 1),), key_rows.shape[0])


def per_device(frames, modulation, w_qkv, b_qkv, qk_gain, block_lists):
    inputs = frames.astype(jnp.float32)
    average = jnp.mean(inputs, axis=-1, keepdims=True)
    centred = inputs - average
    variance = jnp.mean(centred * centred, axis=-1, keepdims=True)
    normed = centred * lax.rsqrt(variance + 1e-06) * (1.0 + modulation[0]) + modulation[1]
    normed = normed.astype(jnp.bfloat16)
    tokens = normed.shape[0]
    width_cols = w_qkv.shape[2]
    head_dim = qk_gain.shape[1]
    heads = width_cols // head_dim
    projected = jnp.einsum(
        "td,djc->tjc",
        normed,
        lax.all_gather(w_qkv, "seq", axis=0, tiled=True),
        preferred_element_type=jnp.float32,
    )
    projected = projected + b_qkv
    queries = normed_heads(projected[:, 0], qk_gain[0], head_dim)
    key_rows = normed_heads(projected[:, 1], qk_gain[1], head_dim)
    values = projected[:, 2].astype(jnp.bfloat16).reshape(tokens, heads, head_dim)
    neighbourhood = reach_sides(key_rows, values)
    position = lax.axis_index("seq")
    tile_dev = block_lists.shape[0]
    tile_len = tokens // tile_dev
    candidates = (position - 1) * tile_dev + jnp.arange(3 * tile_dev, dtype=jnp.int32)
    matches = (block_lists[:, :, None] == candidates[None, None, :]) & (
        block_lists[:, :, None] >= 0
    )
    allowed_tiles = jnp.any(matches, axis=1)
    allowed_keys = jnp.repeat(jnp.repeat(allowed_tiles, tile_len, axis=0), tile_len, axis=1)
    factor = 1.0 / math.sqrt(head_dim)
    scores = (
        jnp.einsum("qhd,khd->hqk", queries, neighbourhood[0], preferred_element_type=jnp.float32)
        * factor
    )
    weights = jnp.where(allowed_keys[None, :, :], jnp.exp(scores), 0.0)
    totals = jnp.sum(weights, axis=-1)
    mixture = jnp.einsum(
        "hqk,khd->qhd",
        weights.astype(jnp.bfloat16),
        neighbourhood[1],
        preferred_element_type=jnp.float32,
    )
    result = (mixture / jnp.transpose(totals)[:, :, None]).astype(jnp.bfloat16)
    return result.reshape(tokens, width_cols)


def solution(mesh):
    placed = (
        P(("groups", "seq"), None),
        P("groups", None),
        P("seq", None, ("fsdp", "head")),
        P(None, ("fsdp", "head")),
        P(),
        P(("groups", "seq"), None),
    )
    return jax.shard_map(
        per_device,
        mesh=mesh,
        in_specs=placed,
        out_specs=P(("groups", "seq"), ("fsdp", "head")),
        check_vma=False,
    )
```

profile of v0, /device:TPU:0, one launch (start us, length us, event | category | flops | bytes accessed | tf_op | source)
XLA Modules:
  0.0 278.2 jit_solution(9089081699902757114)
XLA Ops:
  6.5 0.0 copy-start.6
  6.5 0.0 all-gather.2.cloned.1.call-start
  6.5 4.3 %copy.27 = bf16[768,3,512]{0,2,1:T(8,128)(2,1)} copy(bf16[768,3,512]{2,0,1:T(8,128)(2,1)} %param.8) | data formatting | bytes 4718592 | tf_op args[2]
  10.8 0.0 all-gather.2.cloned.1.call-update
  10.9 0.0 copy-done.6
  10.9 0.0 copy-start
  10.9 0.0 copy-start.5
  10.9 0.0 copy-start.8
  10.9 3.2 %convert_reduce_fusion = f32[768]{0:T(1024)S(1)} fusion(bf16[768,3072]{1,0:T(8,128)(2,1)} %param.6), kind=kLoop, calls=%fused_computation.6 | loop fusion | flops 4717824 | bytes 4721664 | tf_op jit(solution)/shard_map/reduce_sum | solution.py:36
  14.1 0.5 copy-done
  14.6 1.4 fusion.7
  16.0 0.0 copy-done.5
  16.0 164.5 %all-gather.2.cloned.1.call-done = bf16[3072,3,512]{0,2,1:T(8,128)(2,1)} async-done(((bf16[768,3,512]{0,2,1:T(8,128)(2,1)}), bf16[3072,3,512]{0,2,1:T(8,128)(2,1)}) %all-gather.2.cloned.1.call-update) | async-done | bytes 9437200 | tf_op jit(solution)/shard_map/all_gather | solution.py:48
  180.5 0.0 copy-done.8
  180.5 11.9 %broadcast_add_fusion = f32[768,3,512]{0,2,1:T(8,128)S(1)} fusion(f32[3,512]{1,0:T(4,128)S(1)} %copy-done.8, bf16[3072,3,512]{0,2,1:T(8,128)(2,1)} %all-gather.2.cloned.1.call-done, bf16[768,3072]{1,0:T(8,128)(2,1)} %param.6, f32[3072]{0:T(1024)S(1)} %bitcast.43, f32[3072]{0:T(1024)S(1)} %bitcast.42, f32[768]{0:T(1024)S(1)} %add_rsqrt_fusion.2, ...), kind=kOutput, calls=%fused_computation.23 | convolution fusion | flops 7263092736 | bytes 18911232 | tf_op jit(solution)/shard_map/td,djc->tjc/dot_general | solution.py:45
  192.4 0.1 slice.53
  192.5 2.0 fusion.28
  194.5 0.4 copy.29
  194.9 1.5 reduce_sum.47
  196.4 0.0 copy-start.7
  196.4 3.0 %copy.28 = f32[1,768,4,128]{3,1,2,0:T(8,128)} copy(f32[1,768,4,128]{1,3,2,0:T(8,128)} %bitcast.37) | data formatting | bytes 3145728 | tf_op jit(solution)/shard_map/reshape;squeeze | solution.py:22
  199.5 1.9 multiply_convert_fusion.1
  201.4 1.3 pad_maximum_fusion.1
  202.6 1.3 collective-permute-start.1
  203.9 5.7 %collective-permute-start = (bf16[2,768,4,128]{3,1,2,0:T(8,128)(2,1)}, bf16[2,768,4,128]{3,1,2,0:T(8,128)(2,1)}, u32[]{:S(2)}, u32[]{:S(2)}) collective-permute-start(bf16[2,768,4,128]{3,1,2,0:T(8,128)(2,1)} %pad_maximum_fusion.1), channel_id=1, source_target_pairs={{0,4},{4,8},{8,12},{1,5},{5,9},{9,13},{2,6},{6,10},{10,14},{3,7},{... | collective-permute-start | bytes 4718600 | tf_op jit(solution)/shard_map/ppermute | solution.py:15
  209.7 0.0 copy-done.7
  209.7 0.2 and_reduce_fusion
  209.9 0.1 broadcast_in_dim.14
  209.9 1.7 broadcast_in_dim.19
  211.6 5.4 %copy.30 = pred[768,2304]{1,0:T(8,128)(4,1)} copy(pred[768,2304]{0,1:T(8,128)(4,1)} %bitcast.36) | data formatting | bytes 3538944 | tf_op jit(solution)/shard_map/jit(_where)/broadcast_in_dim | solution.py:70
  217.0 1.6 copy.31
  218.6 0.1 multiply_reduce_fusion
  218.8 0.0 copy-start.2
  218.8 0.0 copy-start.4
  218.8 22.4 %collective-permute-done.1 = bf16[2,768,4,128]{3,1,2,0:T(8,128)(2,1)} collective-permute-done((bf16[2,768,4,128]{3,1,2,0:T(8,128)(2,1)}, bf16[2,768,4,128]{3,1,2,0:T(8,128)(2,1)}, u32[]{:S(2)}, u32[]{:S(2)}) %collective-permute-start.1) | collective-permute-done | bytes 1572896 | tf_op jit(solution)/shard_map/ppermute | solution.py:16
  241.2 1.2 collective-permute-done
  242.4 2.0 pad_maximum_fusion
  244.4 0.0 copy-start.1
  244.4 0.0 copy-done.2
  244.4 0.0 copy-done.4
  244.4 0.0 copy-start.3
  244.4 12.9 %fusion = (f32[4,768]{1,0:T(4,128)S(1)}, f32[4,768,2304]{2,1,0:T(8,128)}) fusion(pred[768,2304]{1,0:T(8,128)(4,1)S(1)} %copy-done.2, bf16[2,2304,4,128]{3,1,2,0:T(8,128)(2,1)S(1)} %pad_maximum_fusion, f32[768,4,128]{2,0,1:T(8,128)S(1)} %copy-done.4, f32[128]{0:T(128)S(1)} %get-tuple-element.10, f32[768,4]{0,1:T(4,128)S(1)} %add_rsqrt_fusion), kind=kOutput, calls=%fused_computation.1 | convolution fusion | flops 1834349568 | bytes 34038272 | tf_op jit(solution)/shard_map/qhd,khd->hqk/dot_general | solution.py:67
  257.3 0.0 copy-done.1
  257.3 0.0 copy-done.3
  257.3 12.9 %fusion.21 = bf16[768,4,128]{0,2,1:T(8,128)(2,1)S(1)} fusion(f32[768,4]{0,1:T(4,128)S(1)} %bitcast.44, f32[4,768,2304]{2,1,0:T(8,128)} %get-tuple-element.13, pred[768,2304]{1,0:T(8,128)(4,1)S(1)} %copy-done.3, bf16[2,2304,4,128]{3,1,2,0:T(8,128)(2,1)} %copy-done.1), kind=kOutput, calls=%fused_computation.27 | convolution fusion | flops 1833959424 | bytes 33239040 | tf_op jit(solution)/shard_map/hqk,khd->qhd/dot_general | solution.py:72
  270.2 1.2 copy.33
  (8 shorter events, 0.1 us)
Async XLA Ops:
  6.5 4.3 %copy-start.6 = (f32[2,128]{1,0:T(2,128)S(1)}, f32[2,128]{1,0:T(2,128)}, u32[]{:S(2)}) copy-start(f32[2,128]{1,0:T(2,128)} %param.10) | copy-start | bytes 3076
  6.5 174.0 %all-gather.2.cloned.1.call-start = ((), (), s32[]{:S(2)}) async-start(), calls=%async_computation | async-start | bytes 11796480 | tf_op jit(solution)/shard_map/all_gather | solution.py:48
  10.9 3.8 %copy-start = (bf16[768,3072]{1,0:T(8,128)(2,1)S(1)}, bf16[768,3072]{1,0:T(8,128)(2,1)}, u32[]{:S(2)}) copy-start(bf16[768,3072]{1,0:T(8,128)(2,1)} %param.6) | copy-start | bytes 14155780
  10.9 5.1 %copy-start.5 = (f32[2,3072]{1,0:T(2,128)S(1)}, f32[2,3072]{1,0:T(2,128)}, u32[]{:S(2)}) copy-start(f32[2,3072]{1,0:T(2,128)} %param.7) | copy-start | bytes 73732
  10.9 169.6 %copy-start.8 = (f32[3,512]{1,0:T(4,128)S(1)}, f32[3,512]{1,0:T(4,128)}, u32[]{:S(2)}) copy-start(f32[3,512]{1,0:T(4,128)} %param.9) | copy-start | bytes 18436
  196.4 13.3 %copy-start.7 = (s32[2,27]{1,0:T(2,128)S(1)}, s32[2,27]{1,0:T(2,128)}, u32[]{:S(2)}) copy-start(s32[2,27]{1,0:T(2,128)} %param.11) | copy-start | bytes 652
  202.6 38.6 %collective-permute-start.1 = (bf16[2,768,4,128]{3,1,2,0:T(8,128)(2,1)}, bf16[2,768,4,128]{3,1,2,0:T(8,128)(2,1)}, u32[]{:S(2)}, u32[]{:S(2)}) collective-permute-start(bf16[2,768,4,128]{3,1,2,0:T(8,128)(2,1)} %pad_maximum_fusion.1), channel_id=1, source_target_pairs={{4,0},{8,4},{12,8},{5,1},{9,5},{13,9},{6,2},{10,6},{14,10},{7,3},{... | collective-permute-start | bytes 4718600 | tf_op jit(solution)/shard_map/ppermute | solution.py:16
  203.9 38.4 %collective-permute-start = (bf16[2,768,4,128]{3,1,2,0:T(8,128)(2,1)}, bf16[2,768,4,128]{3,1,2,0:T(8,128)(2,1)}, u32[]{:S(2)}, u32[]{:S(2)}) collective-permute-start(bf16[2,768,4,128]{3,1,2,0:T(8,128)(2,1)} %pad_maximum_fusion.1), channel_id=1, source_target_pairs={{0,4},{4,8},{8,12},{1,5},{5,9},{9,13},{2,6},{6,10},{10,14},{3,7},{... | collective-permute-start | bytes 4718600 | tf_op jit(solution)/shard_map/ppermute | solution.py:15
  218.8 25.6 %copy-start.2 = (pred[768,2304]{1,0:T(8,128)(4,1)S(1)}, pred[768,2304]{1,0:T(8,128)(4,1)}, u32[]{:S(2)}) copy-start(pred[768,2304]{1,0:T(8,128)(4,1)} %copy.30) | copy-start | bytes 5308420
  218.8 25.6 %copy-start.4 = (f32[768,4,128]{2,0,1:T(8,128)S(1)}, f32[768,4,128]{2,0,1:T(8,128)}, u32[]{:S(2)}) copy-start(f32[768,4,128]{2,0,1:T(8,128)} %copy.31) | copy-start | bytes 4718596
  244.4 12.9 %copy-start.1 = (bf16[2,2304,4,128]{3,1,2,0:T(8,128)(2,1)}, bf16[2,2304,4,128]{3,1,2,0:T(8,128)(2,1)S(1)}, u32[]{:S(2)}) copy-start(bf16[2,2304,4,128]{3,1,2,0:T(8,128)(2,1)S(1)} %pad_maximum_fusion) | copy-start | bytes 14155780
  244.4 12.9 %copy-start.3 = (pred[768,2304]{1,0:T(8,128)(4,1)S(1)}, pred[768,2304]{1,0:T(8,128)(4,1)}, u32[]{:S(2)}) copy-start(pred[768,2304]{1,0:T(8,128)(4,1)} %copy.30) | copy-start | bytes 5308420
Sparse Core Ops, SparseCore 0:
  11.0 169.4 all-gather.1
where the time goes:
time: 279 us; the launch traced here: 278 us
  waiting for transfers between devices  188 us (67%)
  matrix products  37.7 us (14%)
  local copies, waits for them, and re-layouts  18.3 us (7%)
  other arithmetic  13.7 us (5%)
  between operations  13.6 us (5%)
  starting transfers between devices  7 us (3%)
    all_gather x1, waiting for transfers between devices, per_device(): lax.all_gather(w_qkv, 'seq', axis=0, tiled=True)  164 us
    ppermute x1, waiting for transfers between devices, with_halo(): after = lax.ppermute(first, axis, down)  22.4 us
    dot_general x1, matrix products, per_device(): jnp.einsum('qhd,khd->hqk', queries, neighbourhood[0], preferred_element_t...  12.9 us
    dot_general x1, matrix products, per_device(): jnp.einsum('hqk,khd->qhd', weights.astype(jnp.bfloat16), neighbourhood[1]...  12.9 us
    dot_general x1, matrix products, per_device(): jnp.einsum('td,djc->tjc', normed, lax.all_gather(w_qkv, 'seq', axis=0, ti...  11.9 us
    ppermute x1, starting transfers between devices, with_halo(): before = lax.ppermute(last, axis, up)  5.72 us
  transfers between devices with their start and end apart: 3, of which 3 were waited for; matrix products, arithmetic and copies ran while one was open for 5% of the time, Pallas kernels for 0%

commit v1 on v0

--- a/solution.py
+++ b/solution.py
@@ -3,6 +3,22 @@
 import jax.numpy as jnp
 from jax import lax
 from jax.sharding import PartitionSpec as P
+
+
+def product_in_turn(x, axis, dim, term):
+    peers, index, extent = (lax.axis_size(axis), lax.axis_index(axis), x.shape[dim])
+    upward = [(i, (i + 1) % peers) for i in range(peers)]
+    backward = [(i, (i - 1) % peers) for i in range(peers)]
+    half = peers // 2
+    from_left = from_right = x
+    total = term(x, index * extent)
+    for step in range(1, half + 1):
+        from_left = lax.ppermute(from_left, axis, upward)
+        if step < peers - half:
+            from_right = lax.ppermute(from_right, axis, backward)
+            total = total + term(from_right, (index + step) % peers * extent)
+        total = total + term(from_left, (index - step) % peers * extent)
+    return total
 
 
 def with_halo(shard, sides, width):
@@ -42,11 +58,16 @@
     width_cols = w_qkv.shape[2]
     head_dim = qk_gain.shape[1]
     heads = width_cols // head_dim
-    projected = jnp.einsum(
-        "td,djc->tjc",
-        normed,
-        lax.all_gather(w_qkv, "seq", axis=0, tiled=True),
-        preferred_element_type=jnp.float32,
+    projected = product_in_turn(
+        w_qkv,
+        "seq",
+        0,
+        lambda part, start: jnp.einsum(
+            "td,djc->tjc",
+            lax.dynamic_slice_in_dim(normed, start, part.shape[0], axis=1),
+            part,
+            preferred_element_type=jnp.float32,
+        ),
     )
     projected = projected + b_qkv
     queries = normed_heads(projected[:, 0], qk_gain[0], head_dim)

time: 279 us -> 242 us (0.87)
  waiting for transfers between devices: 188 us -> 154 us
  between operations: 13.6 us -> 0.32 us
  starting transfers between devices: 7 us -> 12.2 us
  other arithmetic: 13.7 us -> 18.8 us
    all_gather x1 -> x0, waiting for transfers between devices: 164 us -> none  [per_device(): lax.all_gather(w_qkv, 'seq', axis=0, tiled=True)]
    ppermute x0 -> x3, waiting for transfers between devices: none -> 133 us  [the longest x2 94.9 us: product_in_turn(): from_left = lax.ppermute(from_left, axis, upward)]
    ppermute x0 -> x3, starting transfers between devices: none -> 5.17 us  [the longest x2 3.08 us: product_in_turn(): from_left = lax.ppermute(from_left, axis, upward)]
    convert_element_type x0 -> x1, other arithmetic: none -> 5.13 us  [per_device(): normed = normed.astype(jnp.bfloat16)]
    dot_general x1 -> x4, matrix products: 11.9 us -> 13.4 us  [per_device(): jnp.einsum('td,djc->tjc', lax.dynamic_slice_in_dim(normed, start, part.sh...]
  transfers between devices with their start and end apart: 3 -> 5, of which waited for: 3 -> 5; matrix products, arithmetic and copies ran while one was open for 5% -> 12% of each run, Pallas kernels for 0% -> 0%
where the time goes in v1:
time: 242 us; the launch traced here: 241 us
  waiting for transfers between devices  154 us (64%)
  matrix products  39.2 us (16%)
  other arithmetic  18.8 us (8%)
  local copies, waits for them, and re-layouts  16.3 us (7%)
  starting transfers between devices  12.2 us (5%)
    ppermute x2, waiting for transfers between devices, product_in_turn(): from_left = lax.ppermute(from_left, axis, upward)  94.9 us
    ppermute x1, waiting for transfers between devices, product_in_turn(): from_right = lax.ppermute(from_right, axis, backward)  38.3 us
    ppermute x1, waiting for transfers between devices, with_halo(): after = lax.ppermute(first, axis, down)  19.8 us
    dot_general x4, matrix products, per_device(): jnp.einsum('td,djc->tjc', lax.dynamic_slice_in_dim(normed, start, part.sh...  13.4 us
    dot_general x1, matrix products, per_device(): jnp.einsum('hqk,khd->qhd', weights.astype(jnp.bfloat16), neighbourhood[1]...  12.9 us
    dot_general x1, matrix products, per_device(): jnp.einsum('qhd,khd->hqk', queries, neighbourhood[0], preferred_element_t...  12.8 us
    ppermute x1, starting transfers between devices, with_halo(): before = lax.ppermute(last, axis, up)  5.73 us
    broadcast_in_dim x1, local copies, waits for them, and re-layouts, per_device(): weights = jnp.where(allowed_keys[None, :, :], jnp.exp(scores), 0.0)  5.39 us
  transfers between devices with their start and end apart: 5, of which 5 were waited for; matrix products, arithmetic and copies ran while one was open for 12% of the time, Pallas kernels for 0%

profile of v1, /device:TPU:0, one launch (start us, length us, event | category | flops | bytes accessed | tf_op | source)
XLA Modules:
  0.0 241.0 jit_solution(15746195288642044438)
XLA Ops:
  0.0 2.8 %copy.34 = bf16[768,3,512]{0,2,1:T(8,128)(2,1)S(1)} copy(bf16[768,3,512]{2,0,1:T(8,128)(2,1)} %param.8) | data formatting | bytes 4718592 | tf_op args[2]
  2.9 0.0 copy-start
  2.9 0.0 copy-start.8
  2.9 3.1 %collective-permute-start.1 = (bf16[768,3,512]{0,2,1:T(8,128)(2,1)S(1)}, bf16[768,3,512]{0,2,1:T(8,128)(2,1)}, u32[]{:S(2)}, u32[]{:S(2)}) collective-permute-start(bf16[768,3,512]{0,2,1:T(8,128)(2,1)S(1)} %copy.34), channel_id=1, source_target_pairs={{0,4},{4,8},{8,12},{12,0},{1,5},{5,9},{9,13},{13,1},{2,6},{6,10},{... | collective-permute-start | bytes 7077896 | tf_op jit(solution)/shard_map/ppermute | solution.py:16
  6.0 2.1 collective-permute-start
  8.0 3.0 %convert_reduce_fusion = f32[768]{0:T(1024)S(1)} fusion(bf16[768,3072]{1,0:T(8,128)(2,1)} %param.6), kind=kLoop, calls=%fused_computation.6 | loop fusion | flops 4717824 | bytes 4721664 | tf_op jit(solution)/shard_map/reduce_sum | solution.py:52
  11.1 0.0 copy-done.7
  11.1 0.0 copy-done
  11.1 1.4 fusion.7
  12.5 47.7 %collective-permute-done.1 = bf16[768,3,512]{0,2,1:T(8,128)(2,1)} collective-permute-done((bf16[768,3,512]{0,2,1:T(8,128)(2,1)S(1)}, bf16[768,3,512]{0,2,1:T(8,128)(2,1)}, u32[]{:S(2)}, u32[]{:S(2)}) %collective-permute-start.1) | collective-permute-done | bytes 2359328 | tf_op jit(solution)/shard_map/ppermute | solution.py:16
  60.2 0.0 collective-permute-start.2
  60.2 0.0 copy-done.8
  60.3 0.0 copy-start.2
  60.3 5.1 %fusion.10 = bf16[768,3072]{1,0:T(8,128)(2,1)S(1)} fusion(bf16[768,3072]{1,0:T(8,128)(2,1)} %param.6, f32[3072]{0:T(1024)S(1)} %bitcast.52, f32[3072]{0:T(1024)S(1)} %bitcast.51, f32[768]{0:T(1024)S(1)} %add_rsqrt_fusion.2, f32[768]{0:T(1024)S(1)} %broadcast_multiply_fusion), kind=kLoop, calls=%fused_computation.12 | loop fusion | flops 14155776 | bytes 9467904 | tf_op jit(solution)/shard_map/convert_element_type | solution.py:56
  65.4 0.0 copy-done.2
  65.4 2.0 fusion.18
  67.5 3.7 %fusion.14 = f32[768,3,512]{0,2,1:T(8,128)S(1)} fusion(bf16[768,3,512]{0,2,1:T(8,128)(2,1)} %collective-permute-done.1, bf16[768,3072]{1,0:T(8,128)(2,1)S(1)} %fusion.10, s32[]{:T(128)S(6)} %select_n.35), kind=kOutput, calls=%fused_computation.26 | convolution fusion | flops 1811939328 | bytes 8257540 | tf_op jit(solution)/shard_map/td,djc->tjc/dot_general | solution.py:65
  71.2 0.0 copy-start.6
  71.2 38.3 %collective-permute-done = bf16[768,3,512]{0,2,1:T(8,128)(2,1)} collective-permute-done((bf16[768,3,512]{0,2,1:T(8,128)(2,1)S(1)}, bf16[768,3,512]{0,2,1:T(8,128)(2,1)}, u32[]{:S(2)}, u32[]{:S(2)}) %collective-permute-start) | collective-permute-done | bytes 2359328 | tf_op jit(solution)/shard_map/ppermute | solution.py:18
  109.5 3.7 %fusion.16 = f32[768,3,512]{0,2,1:T(8,128)S(1)} fusion(bf16[768,3,512]{0,2,1:T(8,128)(2,1)} %collective-permute-done, bf16[768,3072]{1,0:T(8,128)(2,1)S(1)} %fusion.10, s32[]{:T(128)S(6)} %select_n.33), kind=kOutput, calls=%fused_computation.28 | convolution fusion | flops 1811939328 | bytes 8257540 | tf_op jit(solution)/shard_map/td,djc->tjc/dot_general | solution.py:65
  113.3 47.2 %collective-permute-done.2 = bf16[768,3,512]{0,2,1:T(8,128)(2,1)} collective-permute-done((bf16[768,3,512]{0,2,1:T(8,128)(2,1)}, bf16[768,3,512]{0,2,1:T(8,128)(2,1)}, u32[]{:S(2)}, u32[]{:S(2)}) %collective-permute-start.2) | collective-permute-done | bytes 2359328 | tf_op jit(solution)/shard_map/ppermute | solution.py:16
  160.5 4.0 %add_add_fusion = f32[768,3,512]{0,2,1:T(8,128)S(1)} fusion(f32[768,3,512]{0,2,1:T(8,128)S(1)} %fusion.14, f32[768,3,512]{0,2,1:T(8,128)S(1)} %fusion.18, f32[768,3,512]{0,2,1:T(8,128)S(1)} %fusion.16, f32[3,512]{1,0:T(4,128)S(1)} %copy-done.6, bf16[768,3,512]{0,2,1:T(8,128)(2,1)} %collective-permute-done.2, bf16[768,3072]{1,0:T(8,128)(2,1)S(1)} %fusion.10, ...), kind=kOutput, calls=%fused_computation.14 | convolution fusion | flops 1816657920 | bytes 22421508 | tf_op jit(solution)/shard_map/td,djc->tjc/dot_general | solution.py:65
  164.5 0.1 slice.53
  164.6 2.0 fusion.34
  166.6 0.4 copy.37
  167.0 1.5 reduce_sum.47
  168.5 0.0 copy-start.9
  168.5 3.0 %copy.36 = f32[1,768,4,128]{3,1,2,0:T(8,128)} copy(f32[1,768,4,128]{1,3,2,0:T(8,128)} %bitcast.47) | data formatting | bytes 3145728 | tf_op jit(solution)/shard_map/reshape;squeeze | solution.py:38
  171.5 1.9 multiply_convert_fusion.1
  173.4 1.5 pad_maximum_fusion.1
  174.9 1.3 collective-permute-start.4
  176.2 5.7 %collective-permute-start.3 = (bf16[2,768,4,128]{3,1,2,0:T(8,128)(2,1)}, bf16[2,768,4,128]{3,1,2,0:T(8,128)(2,1)}, u32[]{:S(2)}, u32[]{:S(2)}) collective-permute-start(bf16[2,768,4,128]{3,1,2,0:T(8,128)(2,1)} %pad_maximum_fusion.1), channel_id=1, source_target_pairs={{0,4},{4,8},{8,12},{1,5},{5,9},{9,13},{2,6},{6,10},{10,14},{3,7},{... | collective-permute-start | bytes 4718600 | tf_op jit(solution)/shard_map/ppermute | solution.py:31
  182.0 0.2 and_reduce_fusion
  182.1 0.1 broadcast_in_dim.14
  182.2 1.7 broadcast_in_dim.19
  183.9 5.4 %copy.38 = pred[768,2304]{1,0:T(8,128)(4,1)} copy(pred[768,2304]{0,1:T(8,128)(4,1)} %bitcast.46) | data formatting | bytes 3538944 | tf_op jit(solution)/shard_map/jit(_where)/broadcast_in_dim | solution.py:91
  189.3 1.6 copy.39
  190.9 0.1 multiply_reduce_fusion
  191.1 19.8 %collective-permute-done.4 = bf16[2,768,4,128]{3,1,2,0:T(8,128)(2,1)} collective-permute-done((bf16[2,768,4,128]{3,1,2,0:T(8,128)(2,1)}, bf16[2,768,4,128]{3,1,2,0:T(8,128)(2,1)}, u32[]{:S(2)}, u32[]{:S(2)}) %collective-permute-start.4) | collective-permute-done | bytes 1572896 | tf_op jit(solution)/shard_map/ppermute | solution.py:32
  210.9 1.2 collective-permute-done.3
  212.1 2.0 pad_maximum_fusion
  214.1 0.0 copy-start.1
  214.1 0.0 copy-done.3
  214.1 0.0 copy-done.5
  214.1 0.0 copy-start.4
  214.1 12.8 %fusion = (f32[4,768]{1,0:T(4,128)S(1)}, f32[4,768,2304]{2,1,0:T(8,128)}) fusion(pred[768,2304]{1,0:T(8,128)(4,1)S(1)} %copy-done.3, bf16[2,2304,4,128]{3,1,2,0:T(8,128)(2,1)S(1)} %pad_maximum_fusion, f32[768,4,128]{2,0,1:T(8,128)S(1)} %copy-done.5, f32[128]{0:T(128)S(1)} %get-tuple-element.10, f32[768,4]{0,1:T(4,128)S(1)} %add_rsqrt_fusion), kind=kOutput, calls=%fused_computation.1 | convolution fusion | flops 1834349568 | bytes 34038272 | tf_op jit(solution)/shard_map/qhd,khd->hqk/dot_general | solution.py:88
  227.0 12.9 %fusion.12 = bf16[768,4,128]{0,2,1:T(8,128)(2,1)S(1)} fusion(f32[768,4]{0,1:T(4,128)S(1)} %bitcast.54, f32[4,768,2304]{2,1,0:T(8,128)} %get-tuple-element.13, pred[768,2304]{1,0:T(8,128)(4,1)S(1)} %copy-done.4, bf16[2,2304,4,128]{3,1,2,0:T(8,128)(2,1)} %copy-done.1), kind=kOutput, calls=%fused_computation.21 | convolution fusion | flops 1833959424 | bytes 33239040 | tf_op jit(solution)/shard_map/hqk,khd->qhd/dot_general | solution.py:93
  239.9 1.2 copy.41
  (15 shorter events, 0.1 us)
Async XLA Ops:
  0.0 11.1 %copy-start.7 = (f32[2,3072]{1,0:T(2,128)S(1)}, f32[2,3072]{1,0:T(2,128)}, u32[]{:S(2)}) copy-start(f32[2,3072]{1,0:T(2,128)} %param.7) | copy-start | bytes 73732
  2.9 8.3 %copy-start = (bf16[768,3072]{1,0:T(8,128)(2,1)S(1)}, bf16[768,3072]{1,0:T(8,128)(2,1)}, u32[]{:S(2)}) copy-start(bf16[768,3072]{1,0:T(8,128)(2,1)} %param.6) | copy-start | bytes 14155780
  2.9 57.4 %copy-start.8 = (f32[2,128]{1,0:T(2,128)S(1)}, f32[2,128]{1,0:T(2,128)}, u32[]{:S(2)}) copy-start(f32[2,128]{1,0:T(2,128)} %param.10) | copy-start | bytes 3076
  2.9 57.3 %collective-permute-start.1 = (bf16[768,3,512]{0,2,1:T(8,128)(2,1)S(1)}, bf16[768,3,512]{0,2,1:T(8,128)(2,1)}, u32[]{:S(2)}, u32[]{:S(2)}) collective-permute-start(bf16[768,3,512]{0,2,1:T(8,128)(2,1)S(1)} %copy.34), channel_id=1, source_target_pairs={{0,4},{4,8},{8,12},{12,0},{1,5},{5,9},{9,13},{13,1},{2,6},{6,10},{... | collective-permute-start | bytes 7077896 | tf_op jit(solution)/shard_map/ppermute | solution.py:16
  6.0 103.6 %collective-permute-start = (bf16[768,3,512]{0,2,1:T(8,128)(2,1)S(1)}, bf16[768,3,512]{0,2,1:T(8,128)(2,1)}, u32[]{:S(2)}, u32[]{:S(2)}) collective-permute-start(bf16[768,3,512]{0,2,1:T(8,128)(2,1)S(1)} %copy.34), channel_id=1, source_target_pairs={{0,12},{4,0},{8,4},{12,8},{1,13},{5,1},{9,5},{13,9},{2,14},{6,2},{... | collective-permute-start | bytes 7077896 | tf_op jit(solution)/shard_map/ppermute | solution.py:18
  60.2 100.3 %collective-permute-start.2 = (bf16[768,3,512]{0,2,1:T(8,128)(2,1)}, bf16[768,3,512]{0,2,1:T(8,128)(2,1)}, u32[]{:S(2)}, u32[]{:S(2)}) collective-permute-start(bf16[768,3,512]{0,2,1:T(8,128)(2,1)} %collective-permute-done.1), channel_id=1, source_target_pairs={{0,4},{4,8},{8,12},{12,0},{1,5},{5,9},{9,13},{13,1},{2,6},{6,10},{... | collective-permute-start | bytes 7077896 | tf_op jit(solution)/shard_map/ppermute | solution.py:16
  60.3 5.2 %copy-start.2 = (bf16[768,3,512]{2,0,1:T(8,128)(2,1)S(1)}, bf16[768,3,512]{2,0,1:T(8,128)(2,1)}, u32[]{:S(2)}) copy-start(bf16[768,3,512]{2,0,1:T(8,128)(2,1)} %param.8) | copy-start | bytes 7077892
  71.2 89.3 %copy-start.6 = (f32[3,512]{1,0:T(4,128)S(1)}, f32[3,512]{1,0:T(4,128)}, u32[]{:S(2)}) copy-start(f32[3,512]{1,0:T(4,128)} %param.9) | copy-start | bytes 18436
  168.5 13.5 %copy-start.9 = (s32[2,27]{1,0:T(2,128)S(1)}, s32[2,27]{1,0:T(2,128)}, u32[]{:S(2)}) copy-start(s32[2,27]{1,0:T(2,128)} %param.11) | copy-start | bytes 652
  174.9 36.0 %collective-permute-start.4 = (bf16[2,768,4,128]{3,1,2,0:T(8,128)(2,1)}, bf16[2,768,4,128]{3,1,2,0:T(8,128)(2,1)}, u32[]{:S(2)}, u32[]{:S(2)}) collective-permute-start(bf16[2,768,4,128]{3,1,2,0:T(8,128)(2,1)} %pad_maximum_fusion.1), channel_id=1, source_target_pairs={{4,0},{8,4},{12,8},{5,1},{9,5},{13,9},{6,2},{10,6},{14,10},{7,3},{... | collective-permute-start | bytes 4718600 | tf_op jit(solution)/shard_map/ppermute | solution.py:32
  176.2 35.9 %collective-permute-start.3 = (bf16[2,768,4,128]{3,1,2,0:T(8,128)(2,1)}, bf16[2,768,4,128]{3,1,2,0:T(8,128)(2,1)}, u32[]{:S(2)}, u32[]{:S(2)}) collective-permute-start(bf16[2,768,4,128]{3,1,2,0:T(8,128)(2,1)} %pad_maximum_fusion.1), channel_id=1, source_target_pairs={{0,4},{4,8},{8,12},{1,5},{5,9},{9,13},{2,6},{6,10},{10,14},{3,7},{... | collective-permute-start | bytes 4718600 | tf_op jit(solution)/shard_map/ppermute | solution.py:31
  191.1 23.0 %copy-start.3 = (pred[768,2304]{1,0:T(8,128)(4,1)S(1)}, pred[768,2304]{1,0:T(8,128)(4,1)}, u32[]{:S(2)}) copy-start(pred[768,2304]{1,0:T(8,128)(4,1)} %copy.38) | copy-start | bytes 5308420
  191.1 23.0 %copy-start.5 = (f32[768,4,128]{2,0,1:T(8,128)S(1)}, f32[768,4,128]{2,0,1:T(8,128)}, u32[]{:S(2)}) copy-start(f32[768,4,128]{2,0,1:T(8,128)} %copy.39) | copy-start | bytes 4718596
  214.1 12.9 %copy-start.1 = (bf16[2,2304,4,128]{3,1,2,0:T(8,128)(2,1)}, bf16[2,2304,4,128]{3,1,2,0:T(8,128)(2,1)S(1)}, u32[]{:S(2)}) copy-start(bf16[2,2304,4,128]{3,1,2,0:T(8,128)(2,1)S(1)} %pad_maximum_fusion) | copy-start | bytes 14155780
  214.1 12.9 %copy-start.4 = (pred[768,2304]{1,0:T(8,128)(4,1)S(1)}, pred[768,2304]{1,0:T(8,128)(4,1)}, u32[]{:S(2)}) copy-start(pred[768,2304]{1,0:T(8,128)(4,1)} %copy.38) | copy-start | bytes 5308420
